TPU v7x, 32 devices: a whole 2x2x4 slice. The times are simulated.
32 devices in a mesh: row: 8 (over z, x), col: 4 (over y, core).
Axes of the slice: x: 2, y: 2, z: 4, core: 2. Of those that a mesh axis runs over, the one named last changes fastest.
Arguments:
- covariance: float32 [4096, 4096], P('row', 'col'), may hold values from -6 to 6
- left_ops: float32 [8, 3, 512, 512], P('row', None, None, 'col'), may hold values from -0.15625 to 0.15625
- right_ops: float32 [8, 3, 512, 512], P('col', None, 'row'), may hold values from -0.15625 to 0.15625
- edge_rows: float32 [2, 512, 4096], P(None, 'row', 'col'), may hold values from -6 to 6
- edge_cols: float32 [4096, 2, 512], P('row', None, 'col'), may hold values from -6 to 6
Outputs:
- forecast: float32 [4096, 4096], P('row', 'col')
All inputs are finite; a program needn't handle non-finite values.
Results may differ from a plain program's by a relative error of at most 0.0003.
Values sent between devices are 32-bit elements; how exact they have to be, the bound alone decides.
A program may use at most 64 MiB of HBM per device.

v0:
```python
import jax
import jax.numpy as jnp
from jax import lax
from jax.sharding import PartitionSpec as P


def extended(cells, sides, width):
    for axis, dim in sides:
        count = lax.axis_size(axis)
        ends = count - 1
        head = lax.slice_in_dim(cells, 0, width, axis=dim)
        tail = lax.slice_in_dim(cells, cells.shape[dim] - width, cells.shape[dim], axis=dim)
        cells = jnp.concatenate(
            [
                lax.ppermute(tail, axis, [(i, (i + 1) % count) for i in range(ends)]),
                cells,
                lax.ppermute(head, axis, [((i + 1) % count, i) for i in range(ends)]),
            ],
            axis=dim,
        )
    return cells


def on_device(covariance, left_ops, right_ops, edge_rows, edge_cols):
    row_index = lax.axis_index("row")
    col_index = lax.axis_index("col")
    row_count = lax.axis_size("row")
    col_count = lax.axis_size("col")
    block = covariance.shape[0]
    bands_here = right_ops.shape[0]
    left_full, side_full = (
        lax.all_gather(left_ops, "col", axis=3, tiled=True),
        lax.all_gather(edge_cols[None], "col", axis=3, tiled=True),
    )
    left_blocks = left_full[0]
    sides = side_full[0]
    outside = lax.all_gather(edge_rows, "row", axis=1, tiled=True)
    padded = extended(covariance, (("row", 0),), block)
    upper = jnp.where(row_index == 0, outside[0], padded[:block])
    lower = jnp.where(row_index == row_count - 1, outside[1], padded[2 * block :])
    half = jnp.dot(
        left_blocks[0], upper, preferred_element_type=jnp.float32, precision=lax.Precision.HIGHEST
    )
    half = half + jnp.dot(
        left_blocks[1],
        covariance,
        preferred_element_type=jnp.float32,
        precision=lax.Precision.HIGHEST,
    )
    half = half + jnp.dot(
        left_blocks[2], lower, preferred_element_type=jnp.float32, precision=lax.Precision.HIGHEST
    )
    half_padded = extended(half, (("col", 1),), block)
    before = jnp.where(col_index == 0, sides[:, 0], half_padded[:, :block])
    after = jnp.where(
        col_index == col_count - 1, sides[:, 1], half_padded[:, half_padded.shape[1] - block :]
    )
    cols_ext = jnp.concatenate([before, half, after], axis=1)
    windows = jnp.stack(
        [cols_ext[:, band * block : (band + 3) * block] for band in range(bands_here)]
    )
    windows = windows.reshape(bands_here, block, 3, block)
    result = jnp.einsum(
        "kamb,kmcb->kac",
        windows,
        lax.all_gather(right_ops, "row", axis=2, tiled=True),
        preferred_element_type=jnp.float32,
        precision=lax.Precision.HIGHEST,
    )
    return jnp.transpose(result, (1, 0, 2)).reshape(block, bands_here * block)


def solution(mesh):
    return jax.shard_map(
        on_device,
        mesh=mesh,
        in_specs=(
            P("row", "col"),
            P("row", None, None, "col"),
            P("col", None, "row", None),
            P(None, "row", "col"),
            P("row", None, "col"),
        ),
        out_specs=P("row", "col"),
        check_vma=False,
    )
```

profile of v0, /device:TPU:0, one launch (start us, length us, event | category | flops | bytes accessed | tf_op | source)
XLA Modules:
  0.0 297.6 jit_solution(2806073438769507900)
XLA Ops:
  6.5 0.0 copy-start.2
  6.5 0.0 all-gather.8.cloned.1.call-start
  6.5 0.7 all-gather.8.cloned.1.call-update
  7.3 0.0 all-gather.6.cloned.1.call-start
  7.3 0.7 all-gather.6.cloned.1.call-update
  8.0 0.0 all-gather.12.cloned.1.call-start
  8.1 2.0 copy.6
  10.1 0.0 all-gather.12.cloned.1.call-update
  10.1 0.0 all-gather.10.cloned.1.call-start
  10.2 0.5 all-gather.10.cloned.1.call-update
  10.7 0.0 copy-done.2
  10.7 6.2 %collective-permute-start = (f32[512,1024]{1,0:T(8,128)S(1)}, f32[512,1024]{1,0:T(8,128)}, u32[]{:S(2)}, u32[]{:S(2)}) collective-permute-start(f32[512,1024]{1,0:T(8,128)S(1)} %copy-done.2), channel_id=1, source_target_pairs={{0,4},{4,8},{8,12},{12,16},{16,20},{20,24},{24,28},{1,5},{5,9},{9,... | collective-permute-start | bytes 6291464 | tf_op jit(solution)/shard_map/ppermute | solution.py:15
  16.9 1.3 collective-permute-start.1
  18.2 22.4 %all-gather.8.cloned.1.call-done = f32[1,3,512,512]{3,2,1,0:T(8,128)} async-done(((f32[1,3,512,128]{3,2,1,0:T(8,128)}), f32[1,3,512,512]{3,2,1,0:T(8,128)}) %all-gather.8.cloned.1.call-update) | async-done | bytes 3145744 | tf_op jit(solution)/shard_map/all_gather | solution.py:32
  40.5 6.0 %fusion.13 = f32[512,1024]{0,1:T(8,128)} fusion(f32[512,1024]{1,0:T(8,128)S(1)} %copy-done.2, f32[1,3,512,512]{3,2,1,0:T(8,128)} %all-gather.8.cloned.1.call-done), kind=kOutput, calls=%fused_computation.18 | convolution fusion | flops 3221225472 | bytes 5242880 | tf_op jit(solution)/shard_map/dot_general | solution.py:44
  46.6 84.1 %collective-permute-done = f32[512,1024]{1,0:T(8,128)} collective-permute-done((f32[512,1024]{1,0:T(8,128)S(1)}, f32[512,1024]{1,0:T(8,128)}, u32[]{:S(2)}, u32[]{:S(2)}) %collective-permute-start) | collective-permute-done | bytes 2097184 | tf_op jit(solution)/shard_map/ppermute | solution.py:15
  130.7 20.1 %all-gather.6.cloned.1.call-done = f32[2,512,1024]{2,1,0:T(8,128)} async-done(((f32[2,64,1024]{2,1,0:T(8,128)}), f32[2,512,1024]{2,1,0:T(8,128)}) %all-gather.6.cloned.1.call-update) | async-done | bytes 4194320 | tf_op jit(solution)/shard_map/all_gather | solution.py:37
  150.8 0.0 copy-start
  150.8 0.0 copy-start.1
  150.8 8.9 %fusion.8 = f32[1024,512]{1,0:T(8,128)S(1)} fusion(f32[512,1024]{1,0:T(8,128)} %collective-permute-done, f32[2,512,1024]{2,1,0:T(8,128)} %all-gather.6.cloned.1.call-done, f32[1,3,512,512]{3,2,1,0:T(8,128)} %all-gather.8.cloned.1.call-done, pred[]{:T(512)S(6)} %eq.13), kind=kOutput, calls=%fused_computation.11 | convolution fusion | flops 3221749760 | bytes 7340033 | tf_op jit(solution)/shard_map/dot_general | solution.py:41
  159.7 0.0 collective-permute-done.1
  159.7 0.0 copy-done
  159.7 0.0 copy-done.1
  159.7 8.7 %bitcast_add_fusion = f32[512,1024]{0,1:T(8,128)S(1)} fusion(f32[512,1024]{0,1:T(8,128)S(1)} %copy-done, f32[1024,512]{1,0:T(8,128)S(1)} %fusion.8, f32[512,1024]{1,0:T(8,128)} %collective-permute-done.1, f32[2,512,1024]{2,1,0:T(8,128)S(1)} %copy-done.1, f32[1,3,512,512]{3,2,1,0:T(8,128)} %all-gather.8.cloned.1.call-done, pred[]{:T(512)S(6)} %eq.14), kind=kOutput, calls=%fused_computation.12 | convolution fusion | flops 3222798336 | bytes 11534337 | tf_op jit(solution)/shard_map/dot_general | solution.py:50
  168.4 1.6 fusion.18
  170.0 1.3 collective-permute-start.2
  171.3 1.3 collective-permute-start.3
  172.7 0.8 all-gather.12.cloned.1.call-done
  173.4 0.4 collective-permute-done.2
  173.9 4.1 %collective-permute-done.3 = f32[512,512]{0,1:T(8,128)} collective-permute-done((f32[512,512]{0,1:T(8,128)}, f32[512,512]{0,1:T(8,128)}, u32[]{:S(2)}, u32[]{:S(2)}) %collective-permute-start.3) | collective-permute-done | bytes 1048608 | tf_op jit(solution)/shard_map/ppermute | solution.py:17
  177.9 2.3 fusion.14
  180.3 3.5 %pad_maximum_fusion = (f32[512,1536]{0,1:T(8,128)}, f32[512,1536]{0,1:T(8,128)}) fusion(f32[512,1024]{0,1:T(8,128)S(1)} %bitcast_add_fusion, f32[512,512]{0,1:T(8,128)S(1)} %get-tuple-element.7, f32[512,512]{0,1:T(8,128)S(1)} %get-tuple-element.8), kind=kLoop, calls=%fused_computation.4 | loop fusion | flops 1572864 | bytes 10485760 | tf_op jit(solution)/shard_map/concatenate | solution.py:58
  183.8 2.6 copy.8
  186.4 3.6 %copy.9 = f32[1,512,3,512]{3,1,2,0:T(8,128)} copy(f32[1,512,3,512]{1,3,2,0:T(8,128)} %bitcast.45) | data formatting | bytes 6291456 | tf_op jit(solution)/shard_map/stack | solution.py:59
  190.0 84.1 %all-gather.10.cloned.1.call-done = f32[2,3,512,512]{3,2,1,0:T(8,128)} async-done(((f32[2,3,64,512]{3,2,1,0:T(8,128)}), f32[2,3,512,512]{3,2,1,0:T(8,128)}) %all-gather.10.cloned.1.call-update) | async-done | bytes 6291472 | tf_op jit(solution)/shard_map/all_gather | solution.py:66
  274.1 14.1 %fusion = f32[2,512,512,1]{1,2,3,0:T(8,128)} fusion(f32[2,3,512,512]{3,2,1,0:T(8,128)} %all-gather.10.cloned.1.call-done, f32[1,512,3,512]{3,1,2,0:T(8,128)} %copy.9, f32[1,512,3,512]{3,1,2,0:T(8,128)S(1)} %copy.8), kind=kOutput, calls=%fused_computation | convolution fusion | flops 9665249280 | bytes 14680064 | tf_op jit(solution)/shard_map/kamb,kmcb->kac/dot_general | solution.py:63
  288.2 2.9 copy.10
Async XLA Ops:
  6.5 4.2 %copy-start.2 = (f32[512,1024]{1,0:T(8,128)S(1)}, f32[512,1024]{1,0:T(8,128)}, u32[]{:S(2)}) copy-start(f32[512,1024]{1,0:T(8,128)} %param.5) | copy-start | bytes 6291460
  6.5 34.0 %all-gather.8.cloned.1.call-start = ((), (), s32[]{:S(2)}) async-start(), calls=%async_computation.1 | async-start | bytes 3932160 | tf_op jit(solution)/shard_map/all_gather | solution.py:32
  7.3 143.5 %all-gather.6.cloned.1.call-start = ((), (), s32[]{:S(2)}) async-start(), calls=%async_computation | async-start | bytes 4718592 | tf_op jit(solution)/shard_map/all_gather | solution.py:37
  8.0 165.4 %all-gather.12.cloned.1.call-start = ((), (), s32[]{:S(2)}) async-start(), calls=%async_computation.3 | async-start | bytes 2621440 | tf_op jit(solution)/shard_map/all_gather | solution.py:33
  10.1 264.0 %all-gather.10.cloned.1.call-start = ((), (), s32[]{:S(2)}) async-start(), calls=%async_computation.2 | async-start | bytes 7077888 | tf_op jit(solution)/shard_map/all_gather | solution.py:66
  10.7 120.0 %collective-permute-start = (f32[512,1024]{1,0:T(8,128)S(1)}, f32[512,1024]{1,0:T(8,128)}, u32[]{:S(2)}, u32[]{:S(2)}) collective-permute-start(f32[512,1024]{1,0:T(8,128)S(1)} %copy-done.2), channel_id=1, source_target_pairs={{0,4},{4,8},{8,12},{12,16},{16,20},{20,24},{24,28},{1,5},{5,9},{9,... | collective-permute-start | bytes 6291464 | tf_op jit(solution)/shard_map/ppermute | solution.py:15
  16.9 142.8 %collective-permute-start.1 = (f32[512,1024]{1,0:T(8,128)S(1)}, f32[512,1024]{1,0:T(8,128)}, u32[]{:S(2)}, u32[]{:S(2)}) collective-permute-start(f32[512,1024]{1,0:T(8,128)S(1)} %copy-done.2), channel_id=1, source_target_pairs={{4,0},{8,4},{12,8},{16,12},{20,16},{24,20},{28,24},{5,1},{9,5},{13... | collective-permute-start | bytes 6291464 | tf_op jit(solution)/shard_map/ppermute | solution.py:17
  150.8 8.9 %copy-start = (f32[512,1024]{0,1:T(8,128)S(1)}, f32[512,1024]{0,1:T(8,128)}, u32[]{:S(2)}) copy-start(f32[512,1024]{0,1:T(8,128)} %fusion.13) | copy-start | bytes 6291460
  150.8 8.9 %copy-start.1 = (f32[2,512,1024]{2,1,0:T(8,128)S(1)}, f32[2,512,1024]{2,1,0:T(8,128)}, u32[]{:S(2)}) copy-start(f32[2,512,1024]{2,1,0:T(8,128)} %all-gather.6.cloned.1.call-done) | copy-start | bytes 12582916
  170.0 3.9 %collective-permute-start.2 = (f32[512,512]{0,1:T(8,128)}, f32[512,512]{0,1:T(8,128)S(1)}, u32[]{:S(2)}, u32[]{:S(2)}) collective-permute-start(f32[512,512]{0,1:T(8,128)} %get-tuple-element.9), channel_id=1, source_target_pairs={{0,1},{1,2},{2,3},{4,5},{5,6},{6,7},{8,9},{9,10},{10,11},{12,13},{... | collective-permute-start | bytes 3145736 | tf_op jit(solution)/shard_map/ppermute | solution.py:15
  171.3 6.6 %collective-permute-start.3 = (f32[512,512]{0,1:T(8,128)}, f32[512,512]{0,1:T(8,128)}, u32[]{:S(2)}, u32[]{:S(2)}) collective-permute-start(f32[512,512]{0,1:T(8,128)} %get-tuple-element.10), channel_id=1, source_target_pairs={{1,0},{2,1},{3,2},{5,4},{6,5},{7,6},{9,8},{10,9},{11,10},{13,12},{... | collective-permute-start | bytes 3145736 | tf_op jit(solution)/shard_map/ppermute | solution.py:17
Sparse Core Ops, SparseCore 0:
  8.9 31.6 all-gather.7
  42.7 108.0 all-gather.5
  152.4 21.0 all-gather.11
  175.5 98.6 all-gather.9
where the time goes:
time: 298 us
  waiting for transfers between devices  218 us (73%)
  matrix products  37.7 us (13%)
  between operations  13.2 us (4%)
  local copies, waits for them, and re-layouts  12.7 us (4%)
  starting transfers between devices  10.2 us (3%)
  other arithmetic  5.83 us (2%)
    ppermute x2, waiting for transfers between devices, extended(): lax.ppermute(tail, axis, [(i, (i + 1) % count) for i in range(ends)])  84.5 us
    all_gather x1, waiting for transfers between devices, on_device(): lax.all_gather(right_ops, 'row', axis=2, tiled=True)  84.1 us
    all_gather x1, waiting for transfers between devices, on_device(): lax.all_gather(left_ops, 'col', axis=3, tiled=True)  22.4 us
    all_gather x1, waiting for transfers between devices, on_device(): outside = lax.all_gather(edge_rows, 'row', axis=1, tiled=True)  20.1 us
    dot_general x1, matrix products, on_device(): jnp.einsum('kamb,kmcb->kac', windows, lax.all_gather(right_ops, 'row', ax...  14.1 us
    dot_general x1, matrix products, on_device(): jnp.dot(left_blocks[0], upper, preferred_element_type=jnp.float32, precis...  8.88 us
    dot_general x1, matrix products, on_device(): jnp.dot(left_blocks[2], lower, preferred_element_type=jnp.float32, precis...  8.7 us
    ppermute x2, starting transfers between devices, extended(): lax.ppermute(tail, axis, [(i, (i + 1) % count) for i in range(ends)])  7.52 us
  transfers between devices with their start and end apart: 8, of which 7 were waited for; matrix products, arithmetic and copies ran while one was open for 13% of the time, Pallas kernels for 0%

commit v1 on v0

v1 whole, which is shorter than its diff:
```python
import functools

import jax
import jax.numpy as jnp
from jax import lax
from jax.experimental import pallas as pl
from jax.experimental.pallas import tpu as pltpu
from jax.sharding import PartitionSpec as P

F32, BF16 = jnp.float32, jnp.bfloat16
TILE = 256
CHUNKS = 4


def halves(value):
    high = value.astype(BF16)
    return high, (value - high.astype(F32)).astype(BF16)


def product(a_high, a_low, b_high, b_low, transposed):
    dims = (((1,), (1 if transposed else 0,)), ((), ()))
    dot = functools.partial(lax.dot_general, dimension_numbers=dims, preferred_element_type=F32)
    return dot(a_high, b_high) + (dot(a_high, b_low) + dot(a_low, b_high))


def kernel(
    rows, cols, cov, left, right, edge_r, edge_c, out,
    near, left_all, right_all, edge_all, half, halo, l_high, l_low, w_high, w_low,
    c_send, c_recv, f_send, f_recv, l_send, l_recv, rz_send, rp_send, r_recv, er_send, er_recv,
    ec_send, ec_recv, h_send, h_recv, own_sem,
):
    i, c = lax.axis_index("row"), lax.axis_index("col")
    block = cov.shape[0]
    bands = right.shape[0]
    part = right.shape[2]
    depth = rows // 2
    odd = lax.rem(i, 2)
    pair = i + 1 - 2 * odd
    onward = i + 2 - 4 * odd
    has_onward = (onward >= 0) & (onward < rows)
    fed = (i - 2 + 4 * odd >= 0) & (i - 2 + 4 * odd < rows)
    step_rows = block // CHUNKS

    def remote(src, dst, send, recv, row=None, col=None):
        target = (i if row is None else row, c if col is None else col)
        return pltpu.make_async_remote_copy(
            src_ref=src, dst_ref=dst, send_sem=send, recv_sem=recv,
            device_id=target, device_id_type=pl.DeviceIdType.MESH,
        )

    barrier = pltpu.get_barrier_semaphore()
    for k in range(1, rows):
        pl.semaphore_signal(
            barrier, inc=1, device_id=(lax.rem(i + k, rows), c), device_id_type=pl.DeviceIdType.MESH
        )
    for k in range(1, cols):
        pl.semaphore_signal(
            barrier, inc=1, device_id=(i, lax.rem(c + k, cols)), device_id_type=pl.DeviceIdType.MESH
        )
    pl.semaphore_wait(barrier, rows + cols - 2)

    def piece(j, r):
        return right_all.at[j, :, pl.ds(pl.multiple_of(r * part, part), part), :]

    def cov_copy(k):
        rng = pl.ds(k * step_rows, step_rows)
        return remote(cov.at[rng], near.at[odd, rng], c_send.at[k], c_recv.at[k], row=pair)

    def cov_arrive(k):
        rng = pl.ds(k * step_rows, step_rows)
        return remote(cov.at[rng], near.at[1 - odd, rng], c_send.at[k], c_recv.at[k], row=pair)

    def far_copy(k):
        rng = pl.ds(k * step_rows, step_rows)
        return remote(near.at[1 - odd, rng], near.at[odd, rng], f_send.at[k], f_recv.at[k], row=onward)

    def r_copy_z(j, d, way, r, src):
        return remote(src, piece(j, r), rz_send.at[j, way, d], r_recv.at[j, r], row=i + (2 if way else -2))

    def r_copy_p(j, slot, r, src):
        return remote(src, piece(j, r), rp_send.at[j, slot], r_recv.at[j, r], row=pair)

    for k in range(CHUNKS):
        cov_copy(k).start()
    up, down = i + 2 < rows, i - 2 >= 0
    for j in range(bands):
        @pl.when(up)
        def _():
            r_copy_z(j, 0, 1, i, right.at[j]).start()

        @pl.when(down)
        def _():
            r_copy_z(j, 0, 0, i, right.at[j]).start()

    def l_copy(k):
        return remote(left.at[0], left_all.at[c], l_send.at[k], l_recv.at[c], col=lax.rem(c + k, cols))

    for k in range(1, cols):
        l_copy(k).start()
    er0 = remote(
        edge_r.at[0], near.at[0, pl.ds(pl.multiple_of(i * part, part), part)],
        er_send.at[0], er_recv.at[i], row=0,
    )
    er1 = remote(
        edge_r.at[1], near.at[1, pl.ds(pl.multiple_of(i * part, part), part)],
        er_send.at[1], er_recv.at[i], row=rows - 1,
    )
    ec0 = remote(edge_c.at[0], edge_all.at[c], ec_send.at[0], ec_recv.at[c], col=0)
    ec1 = remote(edge_c.at[1], edge_all.at[c], ec_send.at[1], ec_recv.at[c], col=cols - 1)

    @pl.when(i != 0)
    def _():
        er0.start()

    @pl.when(i != rows - 1)
    def _():
        er1.start()

    @pl.when(c != 0)
    def _():
        ec0.start()

    @pl.when(c != cols - 1)
    def _():
        ec1.start()

    for j in range(bands):
        r_copy_p(j, 0, i, right.at[j]).start()

    own = [pltpu.make_async_copy(left.at[0], left_all.at[c], own_sem.at[0])]
    own += [pltpu.make_async_copy(right.at[j], piece(j, i), own_sem.at[1 + j]) for j in range(bands)]
    for copy in own:
        copy.start()

    @pl.when(i == 0)
    def _():
        near[0, :part] = edge_r[0]

    @pl.when(i == rows - 1)
    def _():
        near[1, (rows - 1) * part :] = edge_r[1]

    @pl.when(c == 0)
    def _():
        edge_all[0] = edge_c[0]

    @pl.when(c == cols - 1)
    def _():
        edge_all[cols - 1] = edge_c[1]

    def pass_on(d):
        for j in range(bands):
            for way in (1, 0):
                r = i - 2 * d if way else i + 2 * d

                @pl.when((r >= 0) & (r < rows))
                def _():
                    r_copy_z(j, d, way, r, piece(j, r)).wait_recv()

                    @pl.when(up if way else down)
                    def _():
                        r_copy_z(j, d, way, r, piece(j, r)).start()

                    r_copy_p(j, 2 * d - way, r, piece(j, r)).start()

    for k in range(CHUNKS):
        cov_arrive(k).wait_recv()

        @pl.when(has_onward)
        def _():
            far_copy(k).start()

        if k == 1 and depth > 1:
            pass_on(1)

    for copy in own:
        copy.wait()
    for k in range(1, cols):
        source = lax.rem(c + k, cols)
        remote(left.at[0], left_all.at[source], l_send.at[k], l_recv.at[source], col=source).wait_recv()
    width = left_all.shape[3]
    for k in range(cols):
        for m in range(3):
            high, low = halves(left_all[k, m])
            l_high[m, :, k * width : (k + 1) * width] = high
            l_low[m, :, k * width : (k + 1) * width] = low

    per_band = block // TILE

    def left_product(m, source, t):
        high, low = halves(source)
        return product(l_high[m], l_low[m], high, low, False)

    def tile_of(t):
        return t // per_band, pl.ds(pl.multiple_of(lax.rem(t, per_band) * TILE, TILE), TILE)

    @pl.loop(0, bands * per_band)
    def _(t):
        band, span = tile_of(t)
        flat = pl.ds(pl.multiple_of(t * TILE, TILE), TILE)
        half[band, :, span] = left_product(1, cov[:, flat], t)

    if depth > 2:
        pass_on(2)

    @pl.loop(0, bands * per_band)
    def _(t):
        band, span = tile_of(t)
        flat = pl.ds(pl.multiple_of(t * TILE, TILE), TILE)
        half[band, :, span] += left_product(2 - 2 * odd, near[1 - odd, :, flat], t)

    @pl.when(fed)
    def _():
        for k in range(CHUNKS):
            rng = pl.ds(k * step_rows, step_rows)
            remote(cov.at[rng], near.at[odd, rng], f_send.at[k], f_recv.at[k], row=pair).wait_recv()

    @pl.when(jnp.logical_not(fed))
    def _():
        for k in range(1, rows):
            source = lax.rem(i + k, rows)
            remote(
                edge_r.at[0], near.at[odd, pl.ds(pl.multiple_of(source * part, part), part)],
                er_send.at[0], er_recv.at[source], row=source,
            ).wait_recv()

    @pl.loop(0, bands * per_band)
    def _(t):
        band, span = tile_of(t)
        flat = pl.ds(pl.multiple_of(t * TILE, TILE), TILE)
        total = half[band, :, span] + left_product(2 * odd, near[odd, :, flat], t)
        half[band, :, span] = total
        high, low = halves(total)
        w_high[band + 1, :, span] = high
        w_low[band + 1, :, span] = low

    to_right = remote(half.at[bands - 1], halo.at[0], h_send.at[0], h_recv.at[0], col=c + 1)
    to_left = remote(half.at[0], halo.at[1], h_send.at[1], h_recv.at[1], col=c - 1)

    @pl.when(c < cols - 1)
    def _():
        to_right.start()

    @pl.when(c > 0)
    def _():
        to_left.start()

    for d in range(3, depth):
        pass_on(d)

    def store_halo(side, inner, copy):
        at = side * (bands + 1)

        @pl.when(inner)
        def _():
            copy.wait_recv()
            high, low = halves(halo[side])
            w_high[at] = high
            w_low[at] = low

        @pl.when(jnp.logical_not(inner))
        def _():
            for k in range(1, cols):
                source = lax.rem(c + k, cols)
                remote(
                    edge_c.at[0], edge_all.at[source], ec_send.at[0], ec_recv.at[source], col=source
                ).wait_recv()
            for k in range(cols):
                high, low = halves(edge_all[k])
                w_high[at, :, k * width : (k + 1) * width] = high
                w_low[at, :, k * width : (k + 1) * width] = low

    store_halo(0, c > 0, to_right)
    store_halo(1, c < cols - 1, to_left)

    for j in range(bands):
        for z in range(depth):
            r = 2 * z + 1 - odd
            r_copy_p(j, 0, r, piece(j, r)).wait_recv()

        @pl.loop(0, per_band)
        def _(t):
            span = pl.ds(pl.multiple_of(t * TILE, TILE), TILE)
            total = None
            for m in range(3):
                high, low = halves(right_all[j, m, span, :])
                term = product(w_high[j + m], w_low[j + m], high, low, True)
                total = term if total is None else total + term
            out[:, pl.ds(pl.multiple_of(j * block + t * TILE, TILE), TILE)] = total

    for k in range(CHUNKS):
        cov_copy(k).wait_send()

        @pl.when(has_onward)
        def _():
            far_copy(k).wait_send()

    for k in range(1, cols):
        l_copy(k).wait_send()
    for j in range(bands):
        r_copy_p(j, 0, i, right.at[j]).wait_send()
        for d in range(depth):
            for way in (1, 0):
                r = i - 2 * d if way else i + 2 * d

                @pl.when((r >= 0) & (r < rows))
                def _():
                    @pl.when(up if way else down)
                    def _():
                        r_copy_z(j, d, way, r, piece(j, r)).wait_send()

                    if d:
                        r_copy_p(j, 2 * d - way, r, piece(j, r)).wait_send()

    @pl.when(i != 0)
    def _():
        er0.wait_send()

    @pl.when(i != rows - 1)
    def _():
        er1.wait_send()

    @pl.when(c != 0)
    def _():
        ec0.wait_send()

    @pl.when(c != cols - 1)
    def _():
        ec1.wait_send()

    @pl.when(c < cols - 1)
    def _():
        to_right.wait_send()

    @pl.when(c > 0)
    def _():
        to_left.wait_send()


def solution(mesh):
    rows, cols = mesh.shape["row"], mesh.shape["col"]

    def on_device(covariance, left_ops, right_ops, edge_rows, edge_cols):
        block = covariance.shape[0]
        bands, _, part, _ = right_ops.shape
        width = left_ops.shape[3]
        edge_cols = jnp.transpose(edge_cols, (1, 0, 2))
        dma = pltpu.SemaphoreType.DMA
        depth = rows // 2
        return pl.pallas_call(
            functools.partial(kernel, rows, cols),
            out_shape=jax.ShapeDtypeStruct(covariance.shape, F32),
            in_specs=[pl.BlockSpec(memory_space=pltpu.VMEM)] * 5,
            out_specs=pl.BlockSpec(memory_space=pltpu.VMEM),
            scratch_shapes=[
                pltpu.VMEM((2,) + covariance.shape, F32),
                pltpu.VMEM((cols, 3, block, width), F32),
                pltpu.VMEM((bands, 3, block, block), F32),
                pltpu.VMEM((cols, block, width), F32),
                pltpu.VMEM((bands, block, block), F32),
                pltpu.VMEM((2, block, block), F32),
                pltpu.VMEM((3, block, block), BF16),
                pltpu.VMEM((3, block, block), BF16),
                pltpu.VMEM((bands + 2, block, block), BF16),
                pltpu.VMEM((bands + 2, block, block), BF16),
                dma((CHUNKS,)), dma((CHUNKS,)), dma((CHUNKS,)), dma((CHUNKS,)),
                dma((cols,)), dma((cols,)),
                dma((bands, 2, depth)), dma((bands, 2 * depth)), dma((bands, rows)),
                dma((2,)), dma((rows,)), dma((2,)), dma((cols,)), dma((2,)), dma((2,)),
                dma((1 + bands,)),
            ],
            compiler_params=pltpu.CompilerParams(
                collective_id=0, has_side_effects=True, vmem_limit_bytes=63 * 1024 * 1024
            ),
        )(covariance, left_ops, right_ops, edge_rows, edge_cols)

    return jax.shard_map(
        on_device,
        mesh=mesh,
        in_specs=(
            P("row", "col"),
            P("row", None, None, "col"),
            P("col", None, "row", None),
            P(None, "row", "col"),
            P("row", None, "col"),
        ),
        out_specs=P("row", "col"),
        check_vma=False,
    )
```

time: 298 us -> 154 us (0.52)
  waiting for transfers between devices: 218 us -> 0 us
  Pallas kernels: 0 us -> 149 us
  matrix products: 37.7 us -> 0 us
  between operations: 13.2 us -> 0.01 us
  starting transfers between devices: 10.2 us -> 0 us
  local copies, waits for them, and re-layouts: 12.7 us -> 5.03 us
  other arithmetic: 5.83 us -> 0 us
    pallas_call x0 -> x1, Pallas kernels: none -> 149 us  [on_device(): pl.pallas_call(functools.partial(kernel, rows, cols), out_shape=jax.Shape...]
    all_gather x4 -> x0, waiting for transfers between devices: 127 us -> none  [the longest x1 84.1 us: on_device(): lax.all_gather(right_ops, 'row', axis=2, tiled=True)]
    ppermute x4 -> x0, waiting for transfers between devices: 88.6 us -> none  [the longest x2 84.5 us: extended(): lax.ppermute(tail, axis, [(i, (i + 1) % count) for i in range(ends)])]
    dot_general x4 -> x0, matrix products: 37.7 us -> none  [the longest x1 14.1 us: on_device(): jnp.einsum('kamb,kmcb->kac', windows, lax.all_gather(right_ops, 'row', ax...]
    ppermute x4 -> x0, starting transfers between devices: 10.1 us -> none  [the longest x2 7.52 us: extended(): lax.ppermute(tail, axis, [(i, (i + 1) % count) for i in range(ends)])]
    another operation x2 -> x0, local copies, waits for them, and re-layouts: 6.2 us -> none  [on_device(): jnp.stack([cols_ext[:, band * block:(band + 3) * block] for band in range...]
    concatenate x1 -> x0, other arithmetic: 3.49 us -> none  [on_device(): cols_ext = jnp.concatenate([before, half, after], axis=1)]
    unnamed x7 -> x2, local copies, waits for them, and re-layouts: 2.04 us -> 5.03 us
  transfers between devices with their start and end apart: 8 -> 0, of which waited for: 7 -> 0; matrix products, arithmetic and copies ran while one was open for 13% -> 0% of each run, Pallas kernels for 0% -> 0%
where the time goes in v1:
time: 154 us
  Pallas kernels  149 us (97%)
  local copies, waits for them, and re-layouts  5.03 us (3%)
    pallas_call x1, Pallas kernels, on_device(): pl.pallas_call(functools.partial(kernel, rows, cols), out_shape=jax.Shape...  149 us
    unnamed x2, local copies, waits for them, and re-layouts  5.03 us

profile of v1, /device:TPU:0, one launch (start us, length us, event | category | flops | bytes accessed | tf_op | source)
XLA Modules:
  0.0 154.2 jit_solution(3811885731382702065)
XLA Ops:
  0.0 1.9 %copy.8 = f32[512,2,128]{2,0,1:T(8,128)} copy(f32[512,2,128]{2,1,0:T(2,128)} %param.9) | data formatting | bytes 1048576 | tf_op args[4]
  1.9 149.2 %shard_map.55 = f32[512,1024]{1,0:T(8,128)} custom-call(f32[512,1024]{1,0:T(8,128)} %cov.1, f32[1,3,512,128]{3,2,1,0:T(8,128)} %left.1, f32[2,3,64,512]{3,2,1,0:T(8,128)} %right.1, f32[2,64,1024]{2,1,0:T(8,128)} %edge_r.1, f32[2,512,128]{2,1,0:T(8,128)} %bitcast.3), custom_call_target="tpu_custom_call" | custom-call | tf_op jit(solution)/shard_map/pallas_call | solution.py:350
  151.1 3.2 %copy.10 = f32[512,1024]{1,0:T(8,128)} copy(f32[512,1024]{1,0:T(8,128)} %shard_map.55) | data formatting | bytes 4194304

commit v2 on v1

--- a/solution.py
+++ b/solution.py
@@ -25,8 +25,8 @@
 
 def kernel(
     rows, cols, cov, left, right, edge_r, edge_c, out,
-    near, left_all, right_all, edge_all, half, halo, l_high, l_low, w_high, w_low,
-    c_send, c_recv, f_send, f_recv, l_send, l_recv, rz_send, rp_send, r_recv, er_send, er_recv,
+    near, left_all, right_all, edge_all, half, halo, relay, l_high, l_low, w_high, w_low,
+    c_send, c_recv, f_send, f_recv, l_send, l_recv, rz_send, rp_send, r_recv, er_send, er_recv, ex_send, ex_recv,
     ec_send, ec_recv, h_send, h_recv, own_sem,
 ):
     i, c = lax.axis_index("row"), lax.axis_index("col")
@@ -83,7 +83,8 @@
     for k in range(CHUNKS):
         cov_copy(k).start()
     up, down = i + 2 < rows, i - 2 >= 0
-    for j in range(bands):
+
+    def own_z(j):
         @pl.when(up)
         def _():
             r_copy_z(j, 0, 1, i, right.at[j]).start()
@@ -91,31 +92,26 @@
         @pl.when(down)
         def _():
             r_copy_z(j, 0, 0, i, right.at[j]).start()
+
+    own_z(0)
+    ex = remote(edge_r.at[1 - odd], relay, ex_send.at[0], ex_recv.at[0], row=pair)
+    ex.start()
+    r_copy_p(0, 0, i, right.at[0]).start()
 
     def l_copy(k):
         return remote(left.at[0], left_all.at[c], l_send.at[k], l_recv.at[c], col=lax.rem(c + k, cols))
 
     for k in range(1, cols):
         l_copy(k).start()
-    er0 = remote(
-        edge_r.at[0], near.at[0, pl.ds(pl.multiple_of(i * part, part), part)],
-        er_send.at[0], er_recv.at[i], row=0,
-    )
-    er1 = remote(
-        edge_r.at[1], near.at[1, pl.ds(pl.multiple_of(i * part, part), part)],
-        er_send.at[1], er_recv.at[i], row=rows - 1,
-    )
+    goal = odd * (rows - 1)
+
+    def edge_copy(k, src, r):
+        dst = near.at[odd, pl.ds(pl.multiple_of(r * part, part), part)]
+        return remote(src, dst, er_send.at[k], er_recv.at[r], row=goal)
+
     ec0 = remote(edge_c.at[0], edge_all.at[c], ec_send.at[0], ec_recv.at[c], col=0)
     ec1 = remote(edge_c.at[1], edge_all.at[c], ec_send.at[1], ec_recv.at[c], col=cols - 1)
 
-    @pl.when(i != 0)
-    def _():
-        er0.start()
-
-    @pl.when(i != rows - 1)
-    def _():
-        er1.start()
-
     @pl.when(c != 0)
     def _():
         ec0.start()
@@ -123,9 +119,6 @@
     @pl.when(c != cols - 1)
     def _():
         ec1.start()
-
-    for j in range(bands):
-        r_copy_p(j, 0, i, right.at[j]).start()
 
     own = [pltpu.make_async_copy(left.at[0], left_all.at[c], own_sem.at[0])]
     own += [pltpu.make_async_copy(right.at[j], piece(j, i), own_sem.at[1 + j]) for j in range(bands)]
@@ -148,30 +141,65 @@
     def _():
         edge_all[cols - 1] = edge_c[1]
 
-    def pass_on(d):
-        for j in range(bands):
-            for way in (1, 0):
-                r = i - 2 * d if way else i + 2 * d
-
-                @pl.when((r >= 0) & (r < rows))
+    def pass_z(d, j):
+        for way in (1, 0):
+            r = i - 2 * d if way else i + 2 * d
+
+            @pl.when((r >= 0) & (r < rows))
+            def _():
+                r_copy_z(j, d, way, r, piece(j, r)).wait_recv()
+
+                @pl.when(up if way else down)
                 def _():
-                    r_copy_z(j, d, way, r, piece(j, r)).wait_recv()
-
-                    @pl.when(up if way else down)
-                    def _():
-                        r_copy_z(j, d, way, r, piece(j, r)).start()
-
-                    r_copy_p(j, 2 * d - way, r, piece(j, r)).start()
-
-    for k in range(CHUNKS):
+                    r_copy_z(j, d, way, r, piece(j, r)).start()
+
+    def pass_x(d, j):
+        for way in (1, 0):
+            r = i - 2 * d if way else i + 2 * d
+
+            @pl.when((r >= 0) & (r < rows))
+            def _():
+                r_copy_p(j, 2 * d - way, r, piece(j, r)).start()
+
+    def cov_on(k):
         cov_arrive(k).wait_recv()
 
         @pl.when(has_onward)
         def _():
             far_copy(k).start()
 
-        if k == 1 and depth > 1:
-            pass_on(1)
+    taken = 0
+    for d in range(1, depth):
+        pass_z(d, 0)
+        pass_x(d, 0)
+        if d == 1:
+            for j in range(1, bands):
+                own_z(j)
+        if d < depth - 1 and taken < CHUNKS - 2:
+            cov_on(taken)
+            taken += 1
+    for j in range(1, bands):
+        r_copy_p(j, 0, i, right.at[j]).start()
+        if depth > 1:
+            pass_z(1, j)
+            pass_x(1, j)
+
+    for k in range(taken, CHUNKS):
+        cov_on(k)
+    ex.wait_recv()
+
+    @pl.when(i != goal)
+    def _():
+        edge_copy(0, edge_r.at[odd], i).start()
+        edge_copy(1, relay, pair).start()
+
+    @pl.when(i == 0)
+    def _():
+        near[0, part : 2 * part] = relay[...]
+
+    @pl.when(i == rows - 1)
+    def _():
+        near[1, (rows - 2) * part : (rows - 1) * part] = relay[...]
 
     for copy in own:
         copy.wait()
@@ -200,8 +228,10 @@
         flat = pl.ds(pl.multiple_of(t * TILE, TILE), TILE)
         half[band, :, span] = left_product(1, cov[:, flat], t)
 
-    if depth > 2:
-        pass_on(2)
+    for j in range(1, bands):
+        if depth > 2:
+            pass_z(2, j)
+            pass_x(2, j)
 
     @pl.loop(0, bands * per_band)
     def _(t):
@@ -217,12 +247,8 @@
 
     @pl.when(jnp.logical_not(fed))
     def _():
-        for k in range(1, rows):
-            source = lax.rem(i + k, rows)
-            remote(
-                edge_r.at[0], near.at[odd, pl.ds(pl.multiple_of(source * part, part), part)],
-                er_send.at[0], er_recv.at[source], row=source,
-            ).wait_recv()
+        for k in range(rows - 2):
+            edge_copy(0, edge_r.at[0], 2 - 2 * odd + k).wait_recv()
 
     @pl.loop(0, bands * per_band)
     def _(t):
@@ -246,7 +272,9 @@
         to_left.start()
 
     for d in range(3, depth):
-        pass_on(d)
+        for j in range(1, bands):
+            pass_z(d, j)
+            pass_x(d, j)
 
     def store_halo(side, inner, copy):
         at = side * (bands + 1)
@@ -312,13 +340,12 @@
                     if d:
                         r_copy_p(j, 2 * d - way, r, piece(j, r)).wait_send()
 
-    @pl.when(i != 0)
-    def _():
-        er0.wait_send()
-
-    @pl.when(i != rows - 1)
-    def _():
-        er1.wait_send()
+    ex.wait_send()
+
+    @pl.when(i != goal)
+    def _():
+        edge_copy(0, edge_r.at[odd], i).wait_send()
+        edge_copy(1, relay, pair).wait_send()
 
     @pl.when(c != 0)
     def _():
@@ -359,6 +386,7 @@
                 pltpu.VMEM((cols, block, width), F32),
                 pltpu.VMEM((bands, block, block), F32),
                 pltpu.VMEM((2, block, block), F32),
+                pltpu.VMEM((part, covariance.shape[1]), F32),
                 pltpu.VMEM((3, block, block), BF16),
                 pltpu.VMEM((3, block, block), BF16),
                 pltpu.VMEM((bands + 2, block, block), BF16),
@@ -366,7 +394,7 @@
                 dma((CHUNKS,)), dma((CHUNKS,)), dma((CHUNKS,)), dma((CHUNKS,)),
                 dma((cols,)), dma((cols,)),
                 dma((bands, 2, depth)), dma((bands, 2 * depth)), dma((bands, rows)),
-                dma((2,)), dma((rows,)), dma((2,)), dma((cols,)), dma((2,)), dma((2,)),
+                dma((2,)), dma((rows,)), dma((1,)), dma((1,)), dma((2,)), dma((cols,)), dma((2,)), dma((2,)),
                 dma((1 + bands,)),
             ],
             compiler_params=pltpu.CompilerParams(

time: 154 us -> 138 us (0.90)
  Pallas kernels: 149 us -> 132 us
    pallas_call x1, Pallas kernels: 149 us -> 132 us  [on_device(): pl.pallas_call(functools.partial(kernel, rows, cols), out_shape=jax.Shape...]
where the time goes in v2:
time: 138 us; the launch traced here: 137 us
  Pallas kernels  132 us (96%)
  local copies, waits for them, and re-layouts  5.03 us (4%)
    pallas_call x1, Pallas kernels, on_device(): pl.pallas_call(functools.partial(kernel, rows, cols), out_shape=jax.Shape...  132 us
    unnamed x2, local copies, waits for them, and re-layouts  5.03 us

profile of v2, /device:TPU:0, one launch (start us, length us, event | category | flops | bytes accessed | tf_op | source)
XLA Modules:
  0.0 137.4 jit_solution(4601800567519656833)
XLA Ops:
  0.0 1.9 %copy.8 = f32[512,2,128]{2,0,1:T(8,128)} copy(f32[512,2,128]{2,1,0:T(2,128)} %param.9) | data formatting | bytes 1048576 | tf_op args[4]
  1.9 132.4 %shard_map.55 = f32[512,1024]{1,0:T(8,128)} custom-call(f32[512,1024]{1,0:T(8,128)} %cov.1, f32[1,3,512,128]{3,2,1,0:T(8,128)} %left.1, f32[2,3,64,512]{3,2,1,0:T(8,128)} %right.1, f32[2,64,1024]{2,1,0:T(8,128)} %edge_r.1, f32[2,512,128]{2,1,0:T(8,128)} %bitcast.3), custom_call_target="tpu_custom_call" | custom-call | tf_op jit(solution)/shard_map/pallas_call | solution.py:377
  134.3 3.2 %copy.10 = f32[512,1024]{1,0:T(8,128)} copy(f32[512,1024]{1,0:T(8,128)} %shard_map.55) | data formatting | bytes 4194304

commit v3 on v2

--- a/solution.py
+++ b/solution.py
@@ -27,7 +27,7 @@
     rows, cols, cov, left, right, edge_r, edge_c, out,
     near, left_all, right_all, edge_all, half, halo, relay, l_high, l_low, w_high, w_low,
     c_send, c_recv, f_send, f_recv, l_send, l_recv, rz_send, rp_send, r_recv, er_send, er_recv, ex_send, ex_recv,
-    ec_send, ec_recv, h_send, h_recv, own_sem,
+    ec_send, ec_recv, h_send, h_recv, sx_send, sz_send, s_recv, own_sem,
 ):
     i, c = lax.axis_index("row"), lax.axis_index("col")
     block = cov.shape[0]
@@ -59,8 +59,27 @@
         )
     pl.semaphore_wait(barrier, rows + cols - 2)
 
+    last = bands - 1
+
+    def span_of(r):
+        return pl.ds(pl.multiple_of(r * part, part), part)
+
     def piece(j, r):
-        return right_all.at[j, :, pl.ds(pl.multiple_of(r * part, part), part), :]
+        return right_all.at[j, pl.ds(0, 2 if j == last else 3), span_of(r), :]
+
+    def own_piece(j):
+        return right.at[j, pl.ds(0, 2 if j == last else 3)]
+
+    def side_piece(r):
+        return right_all.at[last, 2, span_of(r), :]
+
+    def s_copy_z(kind, d, way, r, src):
+        return remote(
+            src, side_piece(r), sz_send.at[kind, way, d], s_recv.at[r], row=i + (2 if way else -2)
+        )
+
+    def s_copy_x(r):
+        return remote(right.at[last, 2], side_piece(r), sx_send.at[0], s_recv.at[r], row=pair)
 
     def cov_copy(k):
         rng = pl.ds(k * step_rows, step_rows)
@@ -87,16 +106,17 @@
     def own_z(j):
         @pl.when(up)
         def _():
-            r_copy_z(j, 0, 1, i, right.at[j]).start()
+            r_copy_z(j, 0, 1, i, own_piece(j)).start()
 
         @pl.when(down)
         def _():
-            r_copy_z(j, 0, 0, i, right.at[j]).start()
+            r_copy_z(j, 0, 0, i, own_piece(j)).start()
 
     own_z(0)
     ex = remote(edge_r.at[1 - odd], relay, ex_send.at[0], ex_recv.at[0], row=pair)
     ex.start()
-    r_copy_p(0, 0, i, right.at[0]).start()
+    r_copy_p(0, 0, i, own_piece(0)).start()
+    s_copy_x(i).start()
 
     def l_copy(k):
         return remote(left.at[0], left_all.at[c], l_send.at[k], l_recv.at[c], col=lax.rem(c + k, cols))
@@ -121,7 +141,7 @@
         ec1.start()
 
     own = [pltpu.make_async_copy(left.at[0], left_all.at[c], own_sem.at[0])]
-    own += [pltpu.make_async_copy(right.at[j], piece(j, i), own_sem.at[1 + j]) for j in range(bands)]
+    own += [pltpu.make_async_copy(right.at[j], right_all.at[j, :, span_of(i)], own_sem.at[1 + j]) for j in range(bands)]
     for copy in own:
         copy.start()
 
@@ -160,6 +180,21 @@
             @pl.when((r >= 0) & (r < rows))
             def _():
                 r_copy_p(j, 2 * d - way, r, piece(j, r)).start()
+
+    def side_z(d):
+        for kind in (0, 1):
+            mine = i if kind == 0 else pair
+            for way in (1, 0):
+                r = mine - 2 * d if way else mine + 2 * d
+
+                @pl.when((r >= 0) & (r < rows))
+                def _():
+                    if d:
+                        s_copy_z(kind, d, way, r, side_piece(r)).wait_recv()
+
+                    @pl.when(up if way else down)
+                    def _():
+                        s_copy_z(kind, d, way, r, right.at[last, 2] if kind + d == 0 else side_piece(r)).start()
 
     def cov_on(k):
         cov_arrive(k).wait_recv()
@@ -179,7 +214,7 @@
             cov_on(taken)
             taken += 1
     for j in range(1, bands):
-        r_copy_p(j, 0, i, right.at[j]).start()
+        r_copy_p(j, 0, i, own_piece(j)).start()
         if depth > 1:
             pass_z(1, j)
             pass_x(1, j)
@@ -201,6 +236,8 @@
     def _():
         near[1, (rows - 2) * part : (rows - 1) * part] = relay[...]
 
+    s_copy_x(pair).wait_recv()
+    side_z(0)
     for copy in own:
         copy.wait()
     for k in range(1, cols):
@@ -275,6 +312,8 @@
         for j in range(1, bands):
             pass_z(d, j)
             pass_x(d, j)
+    if depth > 1:
+        side_z(1)
 
     def store_halo(side, inner, copy):
         at = side * (bands + 1)
@@ -300,11 +339,15 @@
 
     store_halo(0, c > 0, to_right)
     store_halo(1, c < cols - 1, to_left)
+    for d in range(2, depth - 1):
+        side_z(d)
 
     for j in range(bands):
         for z in range(depth):
             r = 2 * z + 1 - odd
             r_copy_p(j, 0, r, piece(j, r)).wait_recv()
+        if j == last and depth > 2:
+            side_z(depth - 1)
 
         @pl.loop(0, per_band)
         def _(t):
@@ -326,7 +369,7 @@
     for k in range(1, cols):
         l_copy(k).wait_send()
     for j in range(bands):
-        r_copy_p(j, 0, i, right.at[j]).wait_send()
+        r_copy_p(j, 0, i, own_piece(j)).wait_send()
         for d in range(depth):
             for way in (1, 0):
                 r = i - 2 * d if way else i + 2 * d
@@ -341,6 +384,17 @@
                         r_copy_p(j, 2 * d - way, r, piece(j, r)).wait_send()
 
     ex.wait_send()
+    s_copy_x(i).wait_send()
+    for d in range(depth):
+        for kind in (0, 1):
+            mine = i if kind == 0 else pair
+            for way in (1, 0):
+                r = mine - 2 * d if way else mine + 2 * d
+
+                @pl.when((r >= 0) & (r < rows) & (up if way else down))
+                def _():
+                    s_copy_z(kind, d, way, r, side_piece(r)).wait_send()
+
 
     @pl.when(i != goal)
     def _():
@@ -395,7 +449,7 @@
                 dma((cols,)), dma((cols,)),
                 dma((bands, 2, depth)), dma((bands, 2 * depth)), dma((bands, rows)),
                 dma((2,)), dma((rows,)), dma((1,)), dma((1,)), dma((2,)), dma((cols,)), dma((2,)), dma((2,)),
-                dma((1 + bands,)),
+                dma((1,)), dma((2, 2, depth)), dma((rows,)), dma((1 + bands,)),
             ],
             compiler_params=pltpu.CompilerParams(
                 collective_id=0, has_side_effects=True, vmem_limit_bytes=63 * 1024 * 1024

time: 138 us -> 129 us (0.935)
  Pallas kernels: 132 us -> 124 us
    pallas_call x1, Pallas kernels: 132 us -> 124 us  [on_device(): pl.pallas_call(functools.partial(kernel, rows, cols), out_shape=jax.Shape...]
where the time goes in v3:
time: 129 us
  Pallas kernels  124 us (96%)
  local copies, waits for them, and re-layouts  5.03 us (4%)
    pallas_call x1, Pallas kernels, on_device(): pl.pallas_call(functools.partial(kernel, rows, cols), out_shape=jax.Shape...  124 us
    unnamed x2, local copies, waits for them, and re-layouts  5.03 us

profile of v3, /device:TPU:0, one launch (start us, length us, event | category | flops | bytes accessed | tf_op | source)
XLA Modules:
  0.0 129.3 jit_solution(16148548718092679334)
XLA Ops:
  0.0 1.9 %copy.8 = f32[512,2,128]{2,0,1:T(8,128)} copy(f32[512,2,128]{2,1,0:T(2,128)} %param.9) | data formatting | bytes 1048576 | tf_op args[4]
  1.9 124.2 %shard_map.55 = f32[512,1024]{1,0:T(8,128)} custom-call(f32[512,1024]{1,0:T(8,128)} %cov.1, f32[1,3,512,128]{3,2,1,0:T(8,128)} %left.1, f32[2,3,64,512]{3,2,1,0:T(8,128)} %right.1, f32[2,64,1024]{2,1,0:T(8,128)} %edge_r.1, f32[2,512,128]{2,1,0:T(8,128)} %bitcast.3), custom_call_target="tpu_custom_call" | custom-call | tf_op jit(solution)/shard_map/pallas_call | solution.py:431
  126.1 3.2 %copy.10 = f32[512,1024]{1,0:T(8,128)} copy(f32[512,1024]{1,0:T(8,128)} %shard_map.55) | data formatting | bytes 4194304

commit v4 on v3

--- a/solution.py
+++ b/solution.py
@@ -25,9 +25,10 @@
 
 def kernel(
     rows, cols, cov, left, right, edge_r, edge_c, out,
+    cov_here, done,
     near, left_all, right_all, edge_all, half, halo, relay, l_high, l_low, w_high, w_low,
     c_send, c_recv, f_send, f_recv, l_send, l_recv, rz_send, rp_send, r_recv, er_send, er_recv, ex_send, ex_recv,
-    ec_send, ec_recv, h_send, h_recv, sx_send, sz_send, s_recv, own_sem,
+    ec_send, ec_recv, h_send, h_recv, sx_send, sz_send, s_recv, own_sem, out_sem,
 ):
     i, c = lax.axis_index("row"), lax.axis_index("col")
     block = cov.shape[0]
@@ -48,6 +49,33 @@
             device_id=target, device_id_type=pl.DeviceIdType.MESH,
         )
 
+    own = [pltpu.make_async_copy(left.at[0], left_all.at[c], own_sem.at[0])]
+    own += [
+        pltpu.make_async_copy(
+            right.at[j],
+            right_all.at[j, :, pl.ds(pl.multiple_of(i * part, part), part)],
+            own_sem.at[1 + j],
+        )
+        for j in range(bands)
+    ]
+    own.append(pltpu.make_async_copy(cov, cov_here, own_sem.at[1 + bands]))
+    for copy in own:
+        copy.start()
+
+    def side_c(k):
+        return edge_c.at[:, k, :]
+
+    edges = (
+        (i == 0, edge_r.at[0], near.at[0, :part]),
+        (i == rows - 1, edge_r.at[1], near.at[1, (rows - 1) * part :]),
+        (c == 0, side_c(0), edge_all.at[0]),
+        (c == cols - 1, side_c(1), edge_all.at[cols - 1]),
+    )
+    for k, (here, src, dst) in enumerate(edges):
+        @pl.when(here)
+        def _():
+            pltpu.make_async_copy(src, dst, own_sem.at[2 + bands + k]).start()
+
     barrier = pltpu.get_barrier_semaphore()
     for k in range(1, rows):
         pl.semaphore_signal(
@@ -129,8 +157,8 @@
         dst = near.at[odd, pl.ds(pl.multiple_of(r * part, part), part)]
         return remote(src, dst, er_send.at[k], er_recv.at[r], row=goal)
 
-    ec0 = remote(edge_c.at[0], edge_all.at[c], ec_send.at[0], ec_recv.at[c], col=0)
-    ec1 = remote(edge_c.at[1], edge_all.at[c], ec_send.at[1], ec_recv.at[c], col=cols - 1)
+    ec0 = remote(side_c(0), edge_all.at[c], ec_send.at[0], ec_recv.at[c], col=0)
+    ec1 = remote(side_c(1), edge_all.at[c], ec_send.at[1], ec_recv.at[c], col=cols - 1)
 
     @pl.when(c != 0)
     def _():
@@ -139,27 +167,6 @@
     @pl.when(c != cols - 1)
     def _():
         ec1.start()
-
-    own = [pltpu.make_async_copy(left.at[0], left_all.at[c], own_sem.at[0])]
-    own += [pltpu.make_async_copy(right.at[j], right_all.at[j, :, span_of(i)], own_sem.at[1 + j]) for j in range(bands)]
-    for copy in own:
-        copy.start()
-
-    @pl.when(i == 0)
-    def _():
-        near[0, :part] = edge_r[0]
-
-    @pl.when(i == rows - 1)
-    def _():
-        near[1, (rows - 1) * part :] = edge_r[1]
-
-    @pl.when(c == 0)
-    def _():
-        edge_all[0] = edge_c[0]
-
-    @pl.when(c == cols - 1)
-    def _():
-        edge_all[cols - 1] = edge_c[1]
 
     def pass_z(d, j):
         for way in (1, 0):
@@ -240,6 +247,11 @@
     side_z(0)
     for copy in own:
         copy.wait()
+    for k, (here, src, dst) in enumerate(edges):
+        @pl.when(here)
+        def _():
+            pltpu.make_async_copy(src, dst, own_sem.at[2 + bands + k]).wait()
+
     for k in range(1, cols):
         source = lax.rem(c + k, cols)
         remote(left.at[0], left_all.at[source], l_send.at[k], l_recv.at[source], col=source).wait_recv()
@@ -263,7 +275,7 @@
     def _(t):
         band, span = tile_of(t)
         flat = pl.ds(pl.multiple_of(t * TILE, TILE), TILE)
-        half[band, :, span] = left_product(1, cov[:, flat], t)
+        half[band, :, span] = left_product(1, cov_here[:, flat], t)
 
     for j in range(1, bands):
         if depth > 2:
@@ -330,7 +342,7 @@
             for k in range(1, cols):
                 source = lax.rem(c + k, cols)
                 remote(
-                    edge_c.at[0], edge_all.at[source], ec_send.at[0], ec_recv.at[source], col=source
+                    side_c(0), edge_all.at[source], ec_send.at[0], ec_recv.at[source], col=source
                 ).wait_recv()
             for k in range(cols):
                 high, low = halves(edge_all[k])
@@ -342,22 +354,36 @@
     for d in range(2, depth - 1):
         side_z(d)
 
+    per_tile = TILE // part
+    late = i >= rows // 2
+
+    def result_copy(j, t):
+        flat = pl.ds(pl.multiple_of(j * block + t * TILE, TILE), TILE)
+        return pltpu.make_async_copy(
+            done.at[:, flat], out.at[:, flat], out_sem.at[j * per_band + t]
+        )
+
     for j in range(bands):
-        for z in range(depth):
-            r = 2 * z + 1 - odd
-            r_copy_p(j, 0, r, piece(j, r)).wait_recv()
         if j == last and depth > 2:
             side_z(depth - 1)
 
         @pl.loop(0, per_band)
-        def _(t):
+        def _(step):
+            t = jnp.where(late, per_band - 1 - step, step)
+
+            @pl.loop(0, per_tile // 2)
+            def _(q):
+                r = t * per_tile + 2 * q + 1 - odd
+                r_copy_p(j, 0, r, piece(j, r)).wait_recv()
+
             span = pl.ds(pl.multiple_of(t * TILE, TILE), TILE)
             total = None
             for m in range(3):
                 high, low = halves(right_all[j, m, span, :])
                 term = product(w_high[j + m], w_low[j + m], high, low, True)
                 total = term if total is None else total + term
-            out[:, pl.ds(pl.multiple_of(j * block + t * TILE, TILE), TILE)] = total
+            done[:, pl.ds(pl.multiple_of(j * block + t * TILE, TILE), TILE)] = total
+            result_copy(j, t).start()
 
     for k in range(CHUNKS):
         cov_copy(k).wait_send()
@@ -383,6 +409,9 @@
                     if d:
                         r_copy_p(j, 2 * d - way, r, piece(j, r)).wait_send()
 
+    for j in range(bands):
+        for t in range(per_band):
+            result_copy(j, t).wait()
     ex.wait_send()
     s_copy_x(i).wait_send()
     for d in range(depth):
@@ -425,15 +454,16 @@
         block = covariance.shape[0]
         bands, _, part, _ = right_ops.shape
         width = left_ops.shape[3]
-        edge_cols = jnp.transpose(edge_cols, (1, 0, 2))
         dma = pltpu.SemaphoreType.DMA
         depth = rows // 2
         return pl.pallas_call(
             functools.partial(kernel, rows, cols),
             out_shape=jax.ShapeDtypeStruct(covariance.shape, F32),
-            in_specs=[pl.BlockSpec(memory_space=pltpu.VMEM)] * 5,
-            out_specs=pl.BlockSpec(memory_space=pltpu.VMEM),
+            in_specs=[pl.BlockSpec(memory_space=pl.ANY)] * 5,
+            out_specs=pl.BlockSpec(memory_space=pl.ANY),
             scratch_shapes=[
+                pltpu.VMEM(covariance.shape, F32),
+                pltpu.VMEM(covariance.shape, F32),
                 pltpu.VMEM((2,) + covariance.shape, F32),
                 pltpu.VMEM((cols, 3, block, width), F32),
                 pltpu.VMEM((bands, 3, block, block), F32),
@@ -449,7 +479,8 @@
                 dma((cols,)), dma((cols,)),
                 dma((bands, 2, depth)), dma((bands, 2 * depth)), dma((bands, rows)),
                 dma((2,)), dma((rows,)), dma((1,)), dma((1,)), dma((2,)), dma((cols,)), dma((2,)), dma((2,)),
-                dma((1,)), dma((2, 2, depth)), dma((rows,)), dma((1 + bands,)),
+                dma((1,)), dma((2, 2, depth)), dma((rows,)), dma((6 + bands,)),
+                dma((bands * block // TILE,)),
             ],
             compiler_params=pltpu.CompilerParams(
                 collective_id=0, has_side_effects=True, vmem_limit_bytes=63 * 1024 * 1024

time: 129 us -> 124 us (0.961)
  Pallas kernels: 124 us -> 120 us
  local copies, waits for them, and re-layouts: 5.03 us -> 3.16 us
    pallas_call x1, Pallas kernels: 124 us -> 120 us  [on_device(): pl.pallas_call(functools.partial(kernel, rows, cols), out_shape=jax.Shape...]
    unnamed x2 -> x1, local copies, waits for them, and re-layouts: 5.03 us -> 3.16 us
where the time goes in v4:
time: 124 us; the launch traced here: 123 us
  Pallas kernels  120 us (97%)
  local copies, waits for them, and re-layouts  3.16 us (3%)
    pallas_call x1, Pallas kernels, on_device(): pl.pallas_call(functools.partial(kernel, rows, cols), out_shape=jax.Shape...  120 us
    unnamed x1, local copies, waits for them, and re-layouts  3.16 us

profile of v4, /device:TPU:0, one launch (start us, length us, event | category | flops | bytes accessed | tf_op | source)
XLA Modules:
  0.0 123.4 jit_solution(15452365257481140779)
XLA Ops:
  0.0 120.2 %shard_map.55 = f32[512,1024]{1,0:T(8,128)} custom-call(f32[512,1024]{1,0:T(8,128)} %cov.1, f32[1,3,512,128]{3,2,1,0:T(8,128)} %left.1, f32[2,3,64,512]{3,2,1,0:T(8,128)} %right.1, f32[2,64,1024]{2,1,0:T(8,128)} %edge_r.1, f32[512,2,128]{2,1,0:T(2,128)} %edge_c.1), custom_call_target="tpu_custom_call" | custom-call | tf_op jit(solution)/shard_map/pallas_call | solution.py:459
  120.2 3.2 %copy.7 = f32[512,1024]{1,0:T(8,128)} copy(f32[512,1024]{1,0:T(8,128)} %shard_map.55) | data formatting | bytes 4194304

commit v5 on v4

--- a/solution.py
+++ b/solution.py
@@ -88,26 +88,35 @@
     pl.semaphore_wait(barrier, rows + cols - 2)
 
     last = bands - 1
+    units = [(j, pl.ds(0, 3)) for j in range(last)] + [(last, pl.ds(0, 1)), (last, pl.ds(1, 1))]
+    count = len(units)
 
     def span_of(r):
         return pl.ds(pl.multiple_of(r * part, part), part)
 
     def piece(j, r):
-        return right_all.at[j, pl.ds(0, 2 if j == last else 3), span_of(r), :]
+        return right_all.at[units[j][0], units[j][1], span_of(r), :]
 
     def own_piece(j):
-        return right.at[j, pl.ds(0, 2 if j == last else 3)]
-
-    def side_piece(r):
-        return right_all.at[last, 2, span_of(r), :]
-
-    def s_copy_z(kind, d, way, r, src):
+        return right.at[units[j][0], units[j][1]]
+
+    def at_end(r):
+        return (r < 2) | (r >= rows - 2)
+
+    def goes(j, r):
+        return jnp.logical_not(at_end(r)) if j == len(units) - 1 else r >= 0
+
+    def side_piece(r, q):
+        return right_all.at[last, 2 - q, span_of(r), :]
+
+    def s_copy_z(kind, d, way, r, src, q):
         return remote(
-            src, side_piece(r), sz_send.at[kind, way, d], s_recv.at[r], row=i + (2 if way else -2)
+            src, side_piece(r, q), sz_send.at[q, kind, way, d], s_recv.at[q, r],
+            row=i + (2 if way else -2),
         )
 
-    def s_copy_x(r):
-        return remote(right.at[last, 2], side_piece(r), sx_send.at[0], s_recv.at[r], row=pair)
+    def s_copy_x(r, q):
+        return remote(right.at[last, 2 - q], side_piece(r, q), sx_send.at[q], s_recv.at[q, r], row=pair)
 
     def cov_copy(k):
         rng = pl.ds(k * step_rows, step_rows)
@@ -132,11 +141,11 @@
     up, down = i + 2 < rows, i - 2 >= 0
 
     def own_z(j):
-        @pl.when(up)
+        @pl.when(up & goes(j, i))
         def _():
             r_copy_z(j, 0, 1, i, own_piece(j)).start()
 
-        @pl.when(down)
+        @pl.when(down & goes(j, i))
         def _():
             r_copy_z(j, 0, 0, i, own_piece(j)).start()
 
@@ -144,7 +153,11 @@
     ex = remote(edge_r.at[1 - odd], relay, ex_send.at[0], ex_recv.at[0], row=pair)
     ex.start()
     r_copy_p(0, 0, i, own_piece(0)).start()
-    s_copy_x(i).start()
+    s_copy_x(i, 0).start()
+
+    @pl.when(at_end(i))
+    def _():
+        s_copy_x(i, 1).start()
 
     def l_copy(k):
         return remote(left.at[0], left_all.at[c], l_send.at[k], l_recv.at[c], col=lax.rem(c + k, cols))
@@ -172,7 +185,7 @@
         for way in (1, 0):
             r = i - 2 * d if way else i + 2 * d
 
-            @pl.when((r >= 0) & (r < rows))
+            @pl.when((r >= 0) & (r < rows) & goes(j, r))
             def _():
                 r_copy_z(j, d, way, r, piece(j, r)).wait_recv()
 
@@ -184,24 +197,26 @@
         for way in (1, 0):
             r = i - 2 * d if way else i + 2 * d
 
-            @pl.when((r >= 0) & (r < rows))
+            @pl.when((r >= 0) & (r < rows) & goes(j, r))
             def _():
                 r_copy_p(j, 2 * d - way, r, piece(j, r)).start()
 
     def side_z(d):
-        for kind in (0, 1):
-            mine = i if kind == 0 else pair
-            for way in (1, 0):
-                r = mine - 2 * d if way else mine + 2 * d
-
-                @pl.when((r >= 0) & (r < rows))
-                def _():
-                    if d:
-                        s_copy_z(kind, d, way, r, side_piece(r)).wait_recv()
-
-                    @pl.when(up if way else down)
+        for q in (0, 1):
+            for kind in (0, 1):
+                mine = i if kind == 0 else pair
+                for way in (1, 0):
+                    r = mine - 2 * d if way else mine + 2 * d
+
+                    @pl.when((r >= 0) & (r < rows) & (at_end(r) if q else r >= 0))
                     def _():
-                        s_copy_z(kind, d, way, r, right.at[last, 2] if kind + d == 0 else side_piece(r)).start()
+                        if d:
+                            s_copy_z(kind, d, way, r, side_piece(r, q), q).wait_recv()
+
+                        @pl.when(up if way else down)
+                        def _():
+                            src = right.at[last, 2 - q] if kind + d == 0 else side_piece(r, q)
+                            s_copy_z(kind, d, way, r, src, q).start()
 
     def cov_on(k):
         cov_arrive(k).wait_recv()
@@ -215,13 +230,16 @@
         pass_z(d, 0)
         pass_x(d, 0)
         if d == 1:
-            for j in range(1, bands):
+            for j in range(1, count):
                 own_z(j)
         if d < depth - 1 and taken < CHUNKS - 2:
             cov_on(taken)
             taken += 1
-    for j in range(1, bands):
-        r_copy_p(j, 0, i, own_piece(j)).start()
+    for j in range(1, count):
+        @pl.when(goes(j, i))
+        def _():
+            r_copy_p(j, 0, i, own_piece(j)).start()
+
         if depth > 1:
             pass_z(1, j)
             pass_x(1, j)
@@ -243,7 +261,12 @@
     def _():
         near[1, (rows - 2) * part : (rows - 1) * part] = relay[...]
 
-    s_copy_x(pair).wait_recv()
+    s_copy_x(pair, 0).wait_recv()
+
+    @pl.when(at_end(i))
+    def _():
+        s_copy_x(pair, 1).wait_recv()
+
     side_z(0)
     for copy in own:
         copy.wait()
@@ -277,7 +300,7 @@
         flat = pl.ds(pl.multiple_of(t * TILE, TILE), TILE)
         half[band, :, span] = left_product(1, cov_here[:, flat], t)
 
-    for j in range(1, bands):
+    for j in range(1, count):
         if depth > 2:
             pass_z(2, j)
             pass_x(2, j)
@@ -321,7 +344,7 @@
         to_left.start()
 
     for d in range(3, depth):
-        for j in range(1, bands):
+        for j in range(1, count):
             pass_z(d, j)
             pass_x(d, j)
     if depth > 1:
@@ -374,7 +397,11 @@
             @pl.loop(0, per_tile // 2)
             def _(q):
                 r = t * per_tile + 2 * q + 1 - odd
-                r_copy_p(j, 0, r, piece(j, r)).wait_recv()
+                for u in range(count):
+                    if units[u][0] == j:
+                        @pl.when(goes(u, r))
+                        def _():
+                            r_copy_p(u, 0, r, piece(u, r)).wait_recv()
 
             span = pl.ds(pl.multiple_of(t * TILE, TILE), TILE)
             total = None
@@ -394,13 +421,16 @@
 
     for k in range(1, cols):
         l_copy(k).wait_send()
-    for j in range(bands):
-        r_copy_p(j, 0, i, own_piece(j)).wait_send()
+    for j in range(count):
+        @pl.when(goes(j, i))
+        def _():
+            r_copy_p(j, 0, i, own_piece(j)).wait_send()
+
         for d in range(depth):
             for way in (1, 0):
                 r = i - 2 * d if way else i + 2 * d
 
-                @pl.when((r >= 0) & (r < rows))
+                @pl.when((r >= 0) & (r < rows) & goes(j, r))
                 def _():
                     @pl.when(up if way else down)
                     def _():
@@ -413,17 +443,23 @@
         for t in range(per_band):
             result_copy(j, t).wait()
     ex.wait_send()
-    s_copy_x(i).wait_send()
-    for d in range(depth):
-        for kind in (0, 1):
-            mine = i if kind == 0 else pair
-            for way in (1, 0):
-                r = mine - 2 * d if way else mine + 2 * d
-
-                @pl.when((r >= 0) & (r < rows) & (up if way else down))
-                def _():
-                    s_copy_z(kind, d, way, r, side_piece(r)).wait_send()
-
+    s_copy_x(i, 0).wait_send()
+
+    @pl.when(at_end(i))
+    def _():
+        s_copy_x(i, 1).wait_send()
+
+    for q in (0, 1):
+        for d in range(depth):
+            for kind in (0, 1):
+                mine = i if kind == 0 else pair
+                for way in (1, 0):
+                    r = mine - 2 * d if way else mine + 2 * d
+                    sent = (r >= 0) & (r < rows) & (up if way else down)
+
+                    @pl.when(sent & at_end(r) if q else sent)
+                    def _():
+                        s_copy_z(kind, d, way, r, side_piece(r, q), q).wait_send()
 
     @pl.when(i != goal)
     def _():
@@ -477,9 +513,9 @@
                 pltpu.VMEM((bands + 2, block, block), BF16),
                 dma((CHUNKS,)), dma((CHUNKS,)), dma((CHUNKS,)), dma((CHUNKS,)),
                 dma((cols,)), dma((cols,)),
-                dma((bands, 2, depth)), dma((bands, 2 * depth)), dma((bands, rows)),
+                dma((bands + 1, 2, depth)), dma((bands + 1, 2 * depth)), dma((bands + 1, rows)),
                 dma((2,)), dma((rows,)), dma((1,)), dma((1,)), dma((2,)), dma((cols,)), dma((2,)), dma((2,)),
-                dma((1,)), dma((2, 2, depth)), dma((rows,)), dma((6 + bands,)),
+                dma((2,)), dma((2, 2, 2, depth)), dma((2, rows)), dma((6 + bands,)),
                 dma((bands * block // TILE,)),
             ],
             compiler_params=pltpu.CompilerParams(

time: 124 us -> 126 us (1.016)
  Pallas kernels: 120 us -> 123 us
    pallas_call x1, Pallas kernels: 120 us -> 123 us  [on_device(): pl.pallas_call(functools.partial(kernel, rows, cols), out_shape=jax.Shape...]
where the time goes in v5:
time: 126 us
  Pallas kernels  123 us (98%)
  local copies, waits for them, and re-layouts  3.16 us (3%)
    pallas_call x1, Pallas kernels, on_device(): pl.pallas_call(functools.partial(kernel, rows, cols), out_shape=jax.Shape...  123 us
    unnamed x1, local copies, waits for them, and re-layouts  3.16 us

profile of v5, /device:TPU:0, one launch (start us, length us, event | category | flops | bytes accessed | tf_op | source)
XLA Modules:
  0.0 125.9 jit_solution(15956345995298330808)
XLA Ops:
  0.0 122.7 %shard_map.55 = f32[512,1024]{1,0:T(8,128)} custom-call(f32[512,1024]{1,0:T(8,128)} %cov.1, f32[1,3,512,128]{3,2,1,0:T(8,128)} %left.1, f32[2,3,64,512]{3,2,1,0:T(8,128)} %right.1, f32[2,64,1024]{2,1,0:T(8,128)} %edge_r.1, f32[512,2,128]{2,1,0:T(2,128)} %edge_c.1), custom_call_target="tpu_custom_call" | custom-call | tf_op jit(solution)/shard_map/pallas_call | solution.py:495
  122.7 3.2 %copy.7 = f32[512,1024]{1,0:T(8,128)} copy(f32[512,1024]{1,0:T(8,128)} %shard_map.55) | data formatting | bytes 4194304

commit v6 on v5

--- a/solution.py
+++ b/solution.py
@@ -343,12 +343,15 @@
     def _():
         to_left.start()
 
+    if depth > 1:
+        side_z(1)
     for d in range(3, depth):
         for j in range(1, count):
             pass_z(d, j)
             pass_x(d, j)
-    if depth > 1:
-        side_z(1)
+
+    for d in range(2, depth - 1):
+        side_z(d)
 
     def store_halo(side, inner, copy):
         at = side * (bands + 1)
@@ -374,8 +377,6 @@
 
     store_halo(0, c > 0, to_right)
     store_halo(1, c < cols - 1, to_left)
-    for d in range(2, depth - 1):
-        side_z(d)
 
     per_tile = TILE // part
     late = i >= rows // 2

time: 126 us -> 126 us (level)
  no operation moved by 1% of the time
where the time goes in v6:
time: 126 us
  Pallas kernels  123 us (98%)
  local copies, waits for them, and re-layouts  3.16 us (3%)
    pallas_call x1, Pallas kernels, on_device(): pl.pallas_call(functools.partial(kernel, rows, cols), out_shape=jax.Shape...  123 us
    unnamed x1, local copies, waits for them, and re-layouts  3.16 us

profile of v6, /device:TPU:0, one launch (start us, length us, event | category | flops | bytes accessed | tf_op | source)
XLA Modules:
  0.0 125.9 jit_solution(12843005793957403831)
XLA Ops:
  0.0 122.7 %shard_map.55 = f32[512,1024]{1,0:T(8,128)} custom-call(f32[512,1024]{1,0:T(8,128)} %cov.1, f32[1,3,512,128]{3,2,1,0:T(8,128)} %left.1, f32[2,3,64,512]{3,2,1,0:T(8,128)} %right.1, f32[2,64,1024]{2,1,0:T(8,128)} %edge_r.1, f32[512,2,128]{2,1,0:T(2,128)} %edge_c.1), custom_call_target="tpu_custom_call" | custom-call | tf_op jit(solution)/shard_map/pallas_call | solution.py:496
  122.7 3.2 %copy.7 = f32[512,1024]{1,0:T(8,128)} copy(f32[512,1024]{1,0:T(8,128)} %shard_map.55) | data formatting | bytes 4194304
